TPU v7x, 32 devices: a whole 2x2x4 slice. The times are simulated.
32 devices in a mesh: op: 4 (over y, x), str: 8 (over z, core).
Axes of the slice: x: 2, y: 2, z: 4, core: 2. Of those that a mesh axis runs over, the one named last changes fastest.
Arguments:
- coeffs: float32 [4096, 4096], P('str'), may hold values from -6 to 6
- previous: float32 [4096, 4096], P('str'), may hold values from -6 to 6
- block_values: bfloat16 [4, 32, 6, 128, 128], P('op'), may hold values from -0.21875 to 0.21875
- block_cols: int32 [4, 32, 6], P('op'), may hold values from 0 to 31, as said below
Outputs:
- advanced: float32 [4096, 4096], P('str')
Inputs may be any that keep to these rules, and one draw needn't show every extreme that they name: For every term k and block row r, block_cols[k, r, 0] equals r and the 6 entries of block_cols[k, r] are distinct.
All inputs are finite; a program needn't handle non-finite values.
Results may differ from a plain program's by a relative error of at most 0.0003.
Values sent between devices are 32-bit elements; how exact they have to be, the bound alone decides.
A program may use at most 192 MiB of HBM per device.

v0:
```python
import math
import jax
import jax.numpy as jnp
from jax import lax
from jax.sharding import PartitionSpec as P

STEPS = 2


def per_device(coeffs, previous, block_values, block_cols):
    local_terms = block_values.shape[0]
    step_scale = 2.0 / math.sqrt(local_terms * lax.axis_size("op"))
    factors = block_values.astype(jnp.float32)
    row_count, full_width = coeffs.shape
    block_size = block_values.shape[-1]
    block_count = full_width // block_size
    slot_count = block_cols.shape[2]
    regrouped = lax.all_to_all(
        previous.reshape(row_count, block_count, block_size),
        "str",
        split_axis=1,
        concat_axis=0,
        tiled=True,
    )
    earlier = regrouped.reshape(full_width, row_count).T
    current = coeffs
    for step_index in range(STEPS):
        column_list = block_cols[0].reshape(-1)
        term_factors = factors[0]
        gathered = jnp.take(
            current.reshape(row_count, block_count, block_size), column_list, axis=1
        )
        gathered = gathered.reshape(row_count, block_count, slot_count, block_size)
        beta_side = jnp.einsum(
            "arjc,rjoc->aro", gathered, term_factors, precision=lax.Precision.HIGHEST
        )
        received = lax.all_to_all(beta_side, "str", split_axis=1, concat_axis=0, tiled=True)
        group_count = received.shape[1]
        item_count = received.shape[2]
        grouped = jnp.take(
            received.reshape(block_count, block_size, group_count, item_count), column_list, axis=0
        )
        grouped = grouped.reshape(block_count, slot_count, block_size, group_count, item_count)
        result = jnp.einsum(
            "rjoc,rjcnm->nmro", term_factors, grouped, precision=lax.Precision.HIGHEST
        )
        moved = result.reshape(group_count, item_count, full_width)
        summed = moved.reshape(row_count, full_width)
        updated = step_scale * lax.psum(summed, "op") - earlier
        earlier, current = (current, updated)
    return current


def solution(mesh):
    placed = (P("str", None), P("str", None), P("op", None, None, None, None), P("op", None, None))
    return jax.shard_map(
        per_device, mesh=mesh, in_specs=placed, out_specs=P("str", None), check_vma=False
    )
```

profile of v0, /device:TPU:0, one launch (start us, length us, event | category | flops | bytes accessed | tf_op | source)
XLA Modules:
  0.0 1236.2 jit_solution(6269851794979325475)
XLA Ops:
  6.5 0.8 copy.25
  7.3 0.1 reshape_squeeze.4
  7.4 9.0 copy.26
  16.4 9.0 copy.27
  25.3 22.2 %gather_fusion = f32[192,512,128]{2,1,0:T(8,128)} fusion(f32[512,32,128]{2,0,1:T(8,128)} %copy.27, s32[1024]{0:T(1024)S(1)} %pad_clamp_fusion), kind=kCustom, calls=%fused_computation.clone | custom fusion | bytes 100664064 | tf_op jit(solution)/shard_map/jit(_take)/gather | solution.py:30
  47.6 34.0 %broadcast_select_fusion.3 = f32[192,512,128]{2,1,0:T(8,128)} fusion(f32[192,512,128]{2,1,0:T(8,128)} %gather_fusion, pred[192]{0:T(512)(128)(4,1)S(1)} %compare_and_fusion), kind=kLoop, calls=%fused_computation.7 | loop fusion | flops 12582912 | bytes 100663488 | tf_op jit(solution)/shard_map/jit(_take)/select_n | solution.py:30
  81.6 30.1 %fusion.8 = f32[512,32,128]{2,0,1:T(8,128)} fusion(f32[512,32,6,128]{3,0,2,1:T(8,128)} %bitcast.92, bf16[1,32,6,128,128]{4,3,2,1,0:T(8,128)(2,1)} %param.10), kind=kOutput, calls=%fused_computation.19 | convolution fusion | flops 19327352832 | bytes 65011712 | tf_op jit(solution)/shard_map/arjc,rjoc->aro/dot_general | solution.py:34
  111.7 6.4 all-to-all-start
  118.1 9.0 copy.31
  127.1 175.0 %all-to-all-done = f32[512,32,128]{2,0,1:T(8,128)} async-done(((f32[512,32,128]{2,0,1:T(8,128)}), f32[512,32,128]{2,0,1:T(8,128)}, u32[]{:S(2)}, u32[]{:S(2)}) %all-to-all-start) | async-done | bytes 8388640 | tf_op jit(solution)/shard_map/all_to_all | solution.py:37
  302.1 4.9 all-to-all-start.1
  307.0 0.0 all-reduce.3.cloned.1.call-start
  307.1 7.7 copy.28
  314.7 22.2 %gather_fusion.1 = f32[192,128,4,128]{3,1,2,0:T(8,128)} fusion(f32[32,128,4,128]{3,1,0,2:T(8,128)} %bitcast.91, s32[1024]{0:T(1024)S(1)} %pad_clamp_fusion), kind=kCustom, calls=%fused_computation.1.clone | custom fusion | bytes 100664064 | tf_op jit(solution)/shard_map/jit(_take)/gather | solution.py:40
  337.0 34.9 %broadcast_select_fusion.1 = f32[192,128,4,128]{3,1,2,0:T(8,128)} fusion(f32[192,128,4,128]{3,1,2,0:T(8,128)} %gather_fusion.1, pred[192]{0:T(512)(128)(4,1)S(1)} %compare_and_fusion), kind=kLoop, calls=%fused_computation.5 | loop fusion | flops 12582912 | bytes 100663488 | tf_op jit(solution)/shard_map/jit(_take)/select_n | solution.py:40
  371.9 48.2 %fusion.14 = f32[4,128,32,128]{3,1,0,2:T(8,128)} fusion(f32[32,6,128,4,128]{4,2,3,1,0:T(8,128)} %bitcast.95, bf16[1,32,6,128,128]{4,3,2,1,0:T(8,128)(2,1)} %param.10), kind=kOutput, calls=%fused_computation.21 | convolution fusion | flops 19327352832 | bytes 65011712 | tf_op jit(solution)/shard_map/rjoc,rjcnm->nmro/dot_general | solution.py:44
  420.1 8.2 copy.30
  428.4 11.7 copy.55
  440.1 0.0 all-reduce.3.cloned.1.call-update
  440.1 0.0 all-reduce.5.cloned.1.call-start
  440.1 50.7 %all-to-all-done.1 = f32[512,32,128]{0,2,1:T(8,128)} async-done(((f32[512,32,128]{0,2,1:T(8,128)}), f32[512,32,128]{0,2,1:T(8,128)}, u32[]{:S(2)}, u32[]{:S(2)}) %all-to-all-start.1) | async-done | bytes 8388640 | tf_op jit(solution)/shard_map/all_to_all | solution.py:18
  490.9 8.4 copy.33
  499.2 11.7 copy.50
  511.0 102.6 %all-reduce.3.cloned.1.call-done = f32[512,4096]{1,0:T(8,128)} async-done(((f32[512,4096]{1,0:T(8,128)}), f32[512,4096]{1,0:T(8,128)}) %all-reduce.3.cloned.1.call-update) | async-done | bytes 8388624 | tf_op jit(solution)/shard_map/psum | solution.py:49
  613.6 11.3 bitcast_subtract_fusion
  624.9 9.0 copy.34
  633.9 8.9 copy.35
  642.8 22.2 %gather_fusion.2 = f32[192,512,128]{2,1,0:T(8,128)} fusion(f32[512,32,128]{2,0,1:T(8,128)} %copy.35, s32[1024]{0:T(1024)S(1)} %pad_clamp_fusion), kind=kCustom, calls=%fused_computation.2.clone | custom fusion | bytes 100664064 | tf_op jit(solution)/shard_map/jit(_take)/gather | solution.py:30
  665.0 34.0 %broadcast_select_fusion.2 = f32[192,512,128]{2,1,0:T(8,128)} fusion(f32[192,512,128]{2,1,0:T(8,128)} %gather_fusion.2, pred[192]{0:T(512)(128)(4,1)S(1)} %compare_and_fusion), kind=kLoop, calls=%fused_computation.6 | loop fusion | flops 12582912 | bytes 100663488 | tf_op jit(solution)/shard_map/jit(_take)/select_n | solution.py:30
  699.1 30.1 %fusion.11 = f32[512,32,128]{2,0,1:T(8,128)} fusion(f32[512,32,6,128]{3,0,2,1:T(8,128)} %bitcast.93, bf16[1,32,6,128,128]{4,3,2,1,0:T(8,128)(2,1)} %param.10), kind=kOutput, calls=%fused_computation.20 | convolution fusion | flops 19327352832 | bytes 65011712 | tf_op jit(solution)/shard_map/arjc,rjoc->aro/dot_general | solution.py:34
  729.2 188.9 %all_to_all.45 = f32[512,32,128]{2,0,1:T(8,128)S(1)} all-to-all(f32[512,32,128]{2,0,1:T(8,128)} %fusion.11), channel_id=1, replica_groups=mesh['op'=4,'str'=8] {'str'}, dimensions={1} | all-to-all | bytes 16777216 | tf_op jit(solution)/shard_map/all_to_all | solution.py:37
  918.1 4.0 copy.36
  922.1 22.2 %gather_fusion.3 = f32[192,128,4,128]{3,1,2,0:T(8,128)} fusion(f32[32,128,4,128]{3,1,0,2:T(8,128)} %bitcast.90, s32[1024]{0:T(1024)S(1)} %pad_clamp_fusion), kind=kCustom, calls=%fused_computation.3.clone | custom fusion | bytes 100664064 | tf_op jit(solution)/shard_map/jit(_take)/gather | solution.py:40
  944.3 34.9 %broadcast_select_fusion = f32[192,128,4,128]{3,1,2,0:T(8,128)} fusion(f32[192,128,4,128]{3,1,2,0:T(8,128)} %gather_fusion.3, pred[192]{0:T(512)(128)(4,1)S(1)} %compare_and_fusion), kind=kLoop, calls=%fused_computation.4 | loop fusion | flops 12582912 | bytes 100663488 | tf_op jit(solution)/shard_map/jit(_take)/select_n | solution.py:40
  979.3 47.8 %fusion.17 = f32[4,128,32,128]{3,1,0,2:T(8,128)} fusion(f32[32,6,128,4,128]{4,2,3,1,0:T(8,128)} %bitcast.94, bf16[1,32,6,128,128]{4,3,2,1,0:T(8,128)(2,1)} %param.10), kind=kOutput, calls=%fused_computation.22 | convolution fusion | flops 19327352832 | bytes 65011712 | tf_op jit(solution)/shard_map/rjoc,rjcnm->nmro/dot_general | solution.py:44
  1027.1 8.2 copy.38
  1035.4 11.8 copy.54
  1047.1 0.0 all-reduce.5.cloned.1.call-update
  1047.1 170.5 %all-reduce.5.cloned.1.call-done = f32[512,4096]{1,0:T(8,128)} async-done(((f32[512,4096]{1,0:T(8,128)}), f32[512,4096]{1,0:T(8,128)}) %all-reduce.5.cloned.1.call-update) | async-done | bytes 8388624 | tf_op jit(solution)/shard_map/psum | solution.py:49
  1217.6 11.3 sub.7
  (3 shorter events, 0.0 us)
Async XLA Ops:
  111.7 190.3 %all-to-all-start = ((f32[512,32,128]{2,0,1:T(8,128)}), f32[512,32,128]{2,0,1:T(8,128)}, u32[]{:S(2)}, u32[]{:S(2)}) async-start(f32[512,32,128]{2,0,1:T(8,128)} %fusion.8), calls=%async_computation | async-start | bytes 16777216 | tf_op jit(solution)/shard_map/all_to_all | solution.py:37
  302.1 188.8 %all-to-all-start.1 = ((f32[512,32,128]{0,2,1:T(8,128)}), f32[512,32,128]{0,2,1:T(8,128)}, u32[]{:S(2)}, u32[]{:S(2)}) async-start(f32[512,32,128]{0,2,1:T(8,128)} %bitcast.97), calls=%async_computation.1 | async-start | bytes 16777216 | tf_op jit(solution)/shard_map/all_to_all | solution.py:18
  307.0 306.5 %all-reduce.3.cloned.1.call-start = ((), (), s32[]{:S(2)}) async-start(), calls=%async_computation.3 | async-start | bytes 16777216 | tf_op jit(solution)/shard_map/psum | solution.py:49
  440.1 777.5 %all-reduce.5.cloned.1.call-start = ((), (), s32[]{:S(2)}) async-start(), calls=%async_computation.4 | async-start | bytes 16777216 | tf_op jit(solution)/shard_map/psum | solution.py:49
Sparse Core Ops, SparseCore 0:
  440.2 173.3 all-reduce.2
  1047.3 170.2 all-reduce.4
where the time goes:
time: 1250 us; the launch traced here: 1240 us
  waiting for transfers between devices  499 us (40%)
  local copies, waits for them, and re-layouts  206 us (16%)
  blocking collectives  189 us (15%)
  other arithmetic  161 us (13%)
  matrix products  156 us (12%)
  between operations  13.9 us (1%)
    psum x2, waiting for transfers between devices, per_device(): updated = step_scale * lax.psum(summed, 'op') - earlier  273 us
    all_to_all x1, blocking collectives, per_device(): lax.all_to_all(beta_side, 'str', split_axis=1, concat_axis=0, tiled=True)  189 us
    all_to_all x1, waiting for transfers between devices, per_device(): lax.all_to_all(beta_side, 'str', split_axis=1, concat_axis=0, tiled=True)  175 us
    dot_general x2, matrix products, per_device(): jnp.einsum('rjoc,rjcnm->nmro', term_factors, grouped, precision=lax.Preci...  96.1 us
    select_n x3, other arithmetic, per_device(): jnp.take(received.reshape(block_count, block_size, group_count, item_coun...  69.9 us
    select_n x2, other arithmetic, per_device(): jnp.take(current.reshape(row_count, block_count, block_size), column_list...  68.1 us
    dot_general x2, matrix products, per_device(): jnp.einsum('arjc,rjoc->aro', gathered, term_factors, precision=lax.Precis...  60.2 us
    unnamed x6, local copies, waits for them, and re-layouts  53.9 us
  transfers between devices with their start and end apart: 4, of which 4 were waited for; matrix products, arithmetic and copies ran while one was open for 13% of the time, Pallas kernels for 0%

commit v1 on v0

--- a/solution.py
+++ b/solution.py
@@ -1,10 +1,38 @@
+import functools
 import math
 import jax
 import jax.numpy as jnp
 from jax import lax
 from jax.sharding import PartitionSpec as P
+from jax.lax import axis_index, axis_size, ppermute
 
 STEPS = 2
+
+
+def face_proceed(state, comm_axis):
+    tile_out, val = (axis_size(comm_axis), axis_index(comm_axis))
+    vec_out = state.shape[1] // tile_out
+    current_value = list(state.shape)
+    current_value[1] = vec_out
+    built = current_value[0]
+    current_value[0] = built * tile_out
+    num = 0
+    x_next = jnp.zeros(current_value, state.dtype)
+    while num < tile_out:
+        later = lax.dynamic_slice_in_dim(state, (val ^ num) * vec_out, vec_out, axis=1)
+        if num:
+            history = []
+            w = 0
+            while w < tile_out:
+                history.append((w, w ^ num))
+                w += 1
+            later = ppermute(later, comm_axis, history)
+        x_next = lax.dynamic_update_slice_in_dim(x_next, later, (val ^ num) * built, axis=0)
+        num += 1
+    return x_next
+
+
+review_runs = functools.partial(face_proceed, comm_axis="str")
 
 
 def per_device(coeffs, previous, block_values, block_cols):
@@ -34,7 +62,7 @@
         beta_side = jnp.einsum(
             "arjc,rjoc->aro", gathered, term_factors, precision=lax.Precision.HIGHEST
         )
-        received = lax.all_to_all(beta_side, "str", split_axis=1, concat_axis=0, tiled=True)
+        received = review_runs(beta_side)
         group_count = received.shape[1]
         item_count = received.shape[2]
         grouped = jnp.take(

time: 1250 us -> 1330 us (1.064)
  waiting for transfers between devices: 499 us -> 723 us
  blocking collectives: 189 us -> 0 us
  local copies, waits for them, and re-layouts: 206 us -> 238 us
    ppermute x0 -> x14, waiting for transfers between devices: none -> 226 us  [face_proceed(): later = ppermute(later, comm_axis, history)]
    all_to_all x1 -> x0, blocking collectives: 189 us -> none  [per_device(): lax.all_to_all(beta_side, 'str', split_axis=1, concat_axis=0, tiled=True)]
    all_to_all x1 -> x0, waiting for transfers between devices: 175 us -> none  [per_device(): lax.all_to_all(beta_side, 'str', split_axis=1, concat_axis=0, tiled=True)]
    psum x2, waiting for transfers between devices: 273 us -> 405 us  [per_device(): updated = step_scale * lax.psum(summed, 'op') - earlier]
    all_to_all x1, waiting for transfers between devices: 50.7 us -> 92.6 us  [per_device(): lax.all_to_all(previous.reshape(row_count, block_count, block_size), 'str...]
    dynamic_update_slice x0 -> x16, local copies, waits for them, and re-layouts: none -> 25.3 us  [face_proceed(): lax.dynamic_update_slice_in_dim(x_next, later, (val ^ num) * built, axis=0)]
    ppermute x0 -> x14, starting transfers between devices: none -> 18.1 us  [face_proceed(): later = ppermute(later, comm_axis, history)]
    unnamed x6 -> x14, local copies, waits for them, and re-layouts: 53.9 us -> 55 us
  transfers between devices with their start and end apart: 4 -> 17, of which waited for: 4 -> 8; matrix products, arithmetic and copies ran while one was open for 13% -> 14% of each run, Pallas kernels for 0% -> 0%
where the time goes in v1:
time: 1330 us; the launch traced here: 1320 us
  waiting for transfers between devices  723 us (54%)
  local copies, waits for them, and re-layouts  238 us (18%)
  other arithmetic  161 us (12%)
  matrix products  156 us (12%)
  starting transfers between devices  23.3 us (2%)
  between operations  14 us (1%)
    psum x2, waiting for transfers between devices, per_device(): updated = step_scale * lax.psum(summed, 'op') - earlier  405 us
    ppermute x14, waiting for transfers between devices, face_proceed(): later = ppermute(later, comm_axis, history)  226 us
    dot_general x2, matrix products, per_device(): jnp.einsum('rjoc,rjcnm->nmro', term_factors, grouped, precision=lax.Preci...  95.9 us
    all_to_all x1, waiting for transfers between devices, per_device(): lax.all_to_all(previous.reshape(row_count, block_count, block_size), 'str...  92.6 us
    select_n x3, other arithmetic, per_device(): jnp.take(received.reshape(block_count, block_size, group_count, item_coun...  69.9 us
    select_n x2, other arithmetic, per_device(): jnp.take(current.reshape(row_count, block_count, block_size), column_list...  68.1 us
    dot_general x2, matrix products, per_device(): jnp.einsum('arjc,rjoc->aro', gathered, term_factors, precision=lax.Precis...  60.4 us
    unnamed x14, local copies, waits for them, and re-layouts  55 us
  transfers between devices with their start and end apart: 17, of which 8 were waited for; matrix products, arithmetic and copies ran while one was open for 14% of the time, Pallas kernels for 0%

profile of v1, /device:TPU:0, one launch (start us, length us, event | category | flops | bytes accessed | tf_op | source)
XLA Modules:
  0.0 1315.8 jit_solution(4811980344420027612)
XLA Ops:
  7.4 9.0 copy.22
  16.4 9.0 copy.23
  25.4 22.3 %gather_fusion = f32[192,512,128]{2,1,0:T(8,128)} fusion(f32[512,32,128]{2,0,1:T(8,128)} %copy.23, s32[1024]{0:T(1024)S(1)} %pad_clamp_fusion), kind=kCustom, calls=%fused_computation.clone | custom fusion | bytes 100664064 | tf_op jit(solution)/shard_map/jit(_take)/gather | solution.py:58
  47.6 34.1 %broadcast_select_fusion.3 = f32[192,512,128]{2,1,0:T(8,128)} fusion(f32[192,512,128]{2,1,0:T(8,128)} %gather_fusion, pred[192]{0:T(512)(128)(4,1)S(1)} %compare_and_fusion), kind=kLoop, calls=%fused_computation.7 | loop fusion | flops 12582912 | bytes 100663488 | tf_op jit(solution)/shard_map/jit(_take)/select_n | solution.py:58
  81.7 30.2 %fusion.8 = f32[32,512,128]{2,1,0:T(8,128)} fusion(f32[512,32,6,128]{3,0,2,1:T(8,128)} %bitcast.112, bf16[1,32,6,128,128]{4,3,2,1,0:T(8,128)(2,1)} %param.10), kind=kOutput, calls=%fused_computation.19 | convolution fusion | flops 19327352832 | bytes 65011712 | tf_op jit(solution)/shard_map/arjc,rjoc->aro/dot_general | solution.py:62
  111.9 5.1 dynamic-slice_bitcast_fusion.7
  117.5 2.6 collective-permute-start.1
  120.1 2.8 collective-permute-start.3
  122.9 3.5 collective-permute-start.5
  126.5 61.9 %collective-permute-done.1 = f32[512,4,128]{2,0,1:T(8,128)S(1)} collective-permute-done((f32[512,4,128]{2,0,1:T(8,128)S(1)}, f32[512,4,128]{2,0,1:T(8,128)S(1)}, u32[]{:S(2)}, u32[]{:S(2)}) %collective-permute-start.1) | collective-permute-done | bytes 1048608 | tf_op jit(solution)/shard_map/ppermute | solution.py:29
  190.1 9.0 copy.26
  199.1 5.0 all-to-all-start
  204.4 3.9 broadcast.9.clone
  212.7 2.3 constant_dynamic-update-slice_fusion.10
  215.0 2.3 constant_dynamic-update-slice_fusion.9
  217.3 42.0 %collective-permute-done.4 = f32[512,4,128]{2,0,1:T(8,128)} collective-permute-done((f32[512,4,128]{2,0,1:T(8,128)S(1)}, f32[512,4,128]{2,0,1:T(8,128)}, u32[]{:S(2)}, u32[]{:S(2)}) %collective-permute-start.4) | collective-permute-done | bytes 1048608 | tf_op jit(solution)/shard_map/ppermute | solution.py:29
  259.2 2.3 constant_dynamic-update-slice_fusion.8
  261.5 2.3 constant_dynamic-update-slice_fusion.7
  263.8 2.3 constant_dynamic-update-slice_fusion.6
  266.0 22.3 %gather_fusion.1 = f32[192,128,4,128]{3,1,2,0:T(8,128)} fusion(f32[32,128,4,128]{3,1,0,2:T(8,128)} %bitcast.14, s32[1024]{0:T(1024)S(1)} %pad_clamp_fusion), kind=kCustom, calls=%fused_computation.1.clone | custom fusion | bytes 100664064 | tf_op jit(solution)/shard_map/jit(_take)/gather | solution.py:68
  288.3 34.9 %broadcast_select_fusion.1 = f32[192,128,4,128]{3,1,2,0:T(8,128)} fusion(f32[192,128,4,128]{3,1,2,0:T(8,128)} %gather_fusion.1, pred[192]{0:T(512)(128)(4,1)S(1)} %compare_and_fusion), kind=kLoop, calls=%fused_computation.5 | loop fusion | flops 12582912 | bytes 100663488 | tf_op jit(solution)/shard_map/jit(_take)/select_n | solution.py:68
  323.2 48.1 %fusion.14 = f32[4,128,32,128]{3,1,0,2:T(8,128)} fusion(f32[32,6,128,4,128]{4,2,3,1,0:T(8,128)} %bitcast.115, bf16[1,32,6,128,128]{4,3,2,1,0:T(8,128)(2,1)} %param.10), kind=kOutput, calls=%fused_computation.21 | convolution fusion | flops 19327352832 | bytes 65011712 | tf_op jit(solution)/shard_map/rjoc,rjcnm->nmro/dot_general | solution.py:72
  371.3 8.2 copy.25
  379.6 11.7 copy.49
  391.3 92.6 %all-to-all-done = f32[512,32,128]{0,2,1:T(8,128)} async-done(((f32[512,32,128]{0,2,1:T(8,128)}), f32[512,32,128]{0,2,1:T(8,128)}, u32[]{:S(2)}, u32[]{:S(2)}) %all-to-all-start) | async-done | bytes 8388640 | tf_op jit(solution)/shard_map/all_to_all | solution.py:46
  484.0 8.2 copy.28
  492.2 11.7 copy.44
  503.9 190.4 %all-reduce.3.cloned.1.call-done = f32[512,4096]{1,0:T(8,128)} async-done(((f32[512,4096]{1,0:T(8,128)}), f32[512,4096]{1,0:T(8,128)}) %all-reduce.3.cloned.1.call-update) | async-done | bytes 8388624 | tf_op jit(solution)/shard_map/psum | solution.py:77
  694.3 11.3 bitcast_subtract_fusion
  705.6 9.0 copy.29
  714.6 8.9 copy.30
  723.6 22.3 %gather_fusion.2 = f32[192,512,128]{2,1,0:T(8,128)} fusion(f32[512,32,128]{2,0,1:T(8,128)} %copy.30, s32[1024]{0:T(1024)S(1)} %pad_clamp_fusion), kind=kCustom, calls=%fused_computation.2.clone | custom fusion | bytes 100664064 | tf_op jit(solution)/shard_map/jit(_take)/gather | solution.py:58
  745.8 34.1 %broadcast_select_fusion.2 = f32[192,512,128]{2,1,0:T(8,128)} fusion(f32[192,512,128]{2,1,0:T(8,128)} %gather_fusion.2, pred[192]{0:T(512)(128)(4,1)S(1)} %compare_and_fusion), kind=kLoop, calls=%fused_computation.6 | loop fusion | flops 12582912 | bytes 100663488 | tf_op jit(solution)/shard_map/jit(_take)/select_n | solution.py:58
  779.9 30.2 %fusion.11 = f32[32,512,128]{2,1,0:T(8,128)} fusion(f32[512,32,6,128]{3,0,2,1:T(8,128)} %bitcast.113, bf16[1,32,6,128,128]{4,3,2,1,0:T(8,128)(2,1)} %param.10), kind=kOutput, calls=%fused_computation.20 | convolution fusion | flops 19327352832 | bytes 65011712 | tf_op jit(solution)/shard_map/arjc,rjoc->aro/dot_general | solution.py:62
  810.1 3.9 dynamic-slice_bitcast_fusion
  815.9 2.4 collective-permute-start.10
  818.6 3.3 collective-permute-start.12
  821.9 62.5 %collective-permute-done.8 = f32[512,4,128]{2,0,1:T(8,128)S(1)} collective-permute-done((f32[512,4,128]{2,0,1:T(8,128)S(1)}, f32[512,4,128]{2,0,1:T(8,128)S(1)}, u32[]{:S(2)}, u32[]{:S(2)}) %collective-permute-start.8) | collective-permute-done | bytes 1048608 | tf_op jit(solution)/shard_map/ppermute | solution.py:29
  884.5 3.9 broadcast.9
  892.8 13.0 collective-permute-done.9
  907.9 46.1 %collective-permute-done.11 = f32[512,4,128]{2,0,1:T(8,128)S(1)} collective-permute-done((f32[512,4,128]{2,0,1:T(8,128)S(1)}, f32[512,4,128]{2,0,1:T(8,128)S(1)}, u32[]{:S(2)}, u32[]{:S(2)}) %collective-permute-start.11) | collective-permute-done | bytes 1048608 | tf_op jit(solution)/shard_map/ppermute | solution.py:29
  957.2 22.4 %gather_fusion.3 = f32[192,128,4,128]{3,1,2,0:T(8,128)} fusion(f32[32,128,4,128]{3,1,0,2:T(8,128)} %bitcast.39, s32[1024]{0:T(1024)S(1)} %pad_clamp_fusion), kind=kCustom, calls=%fused_computation.3.clone | custom fusion | bytes 100664064 | tf_op jit(solution)/shard_map/jit(_take)/gather | solution.py:68
  979.6 34.9 %broadcast_select_fusion = f32[192,128,4,128]{3,1,2,0:T(8,128)} fusion(f32[192,128,4,128]{3,1,2,0:T(8,128)} %gather_fusion.3, pred[192]{0:T(512)(128)(4,1)S(1)} %compare_and_fusion), kind=kLoop, calls=%fused_computation.4 | loop fusion | flops 12582912 | bytes 100663488 | tf_op jit(solution)/shard_map/jit(_take)/select_n | solution.py:68
  1014.6 47.8 %fusion.17 = f32[4,128,32,128]{3,1,0,2:T(8,128)} fusion(f32[32,6,128,4,128]{4,2,3,1,0:T(8,128)} %bitcast.114, bf16[1,32,6,128,128]{4,3,2,1,0:T(8,128)(2,1)} %param.10), kind=kOutput, calls=%fused_computation.22 | convolution fusion | flops 19327352832 | bytes 65011712 | tf_op jit(solution)/shard_map/rjoc,rjcnm->nmro/dot_general | solution.py:72
  1062.4 8.2 copy.32
  1070.7 11.8 copy.48
  1082.4 214.8 %all-reduce.5.cloned.1.call-done = f32[512,4096]{1,0:T(8,128)} async-done(((f32[512,4096]{1,0:T(8,128)}), f32[512,4096]{1,0:T(8,128)}) %all-reduce.5.cloned.1.call-update) | async-done | bytes 8388624 | tf_op jit(solution)/shard_map/psum | solution.py:77
  1297.3 11.3 sub.7
  (46 shorter events, 19.7 us)
Async XLA Ops:
  117.0 5.9 collective-permute-start
  117.5 70.9 %collective-permute-start.1 = (f32[512,4,128]{2,0,1:T(8,128)S(1)}, f32[512,4,128]{2,0,1:T(8,128)S(1)}, u32[]{:S(2)}, u32[]{:S(2)}) collective-permute-start(f32[512,4,128]{2,0,1:T(8,128)S(1)} %get-tuple-element.19), channel_id=1, source_target_pairs={{0,2},{1,3},{2,0},{3,1},{4,6},{5,7},{6,4},{7,5},{8,10},{9,11},{10,... | collective-permute-start | bytes 3145736 | tf_op jit(solution)/shard_map/ppermute | solution.py:29
  120.0 92.7 %collective-permute-start.2 = (f32[512,4,128]{2,0,1:T(8,128)}, f32[512,4,128]{2,0,1:T(8,128)}, u32[]{:S(2)}, u32[]{:S(2)}) collective-permute-start(f32[512,4,128]{2,0,1:T(8,128)} %get-tuple-element.18), channel_id=1, source_target_pairs={{0,3},{1,2},{2,1},{3,0},{4,7},{5,6},{6,5},{7,4},{8,11},{9,10},{10,... | collective-permute-start | bytes 3145736 | tf_op jit(solution)/shard_map/ppermute | solution.py:29
  120.1 94.9 %collective-permute-start.3 = (f32[512,4,128]{2,0,1:T(8,128)}, f32[512,4,128]{2,0,1:T(8,128)}, u32[]{:S(2)}, u32[]{:S(2)}) collective-permute-start(f32[512,4,128]{2,0,1:T(8,128)} %get-tuple-element.17), channel_id=1, source_target_pairs={{0,4},{1,5},{2,6},{3,7},{4,0},{5,1},{6,2},{7,3},{8,12},{9,13},{10,... | collective-permute-start | bytes 3145736 | tf_op jit(solution)/shard_map/ppermute | solution.py:29
  122.9 136.3 %collective-permute-start.4 = (f32[512,4,128]{2,0,1:T(8,128)S(1)}, f32[512,4,128]{2,0,1:T(8,128)}, u32[]{:S(2)}, u32[]{:S(2)}) collective-permute-start(f32[512,4,128]{2,0,1:T(8,128)S(1)} %get-tuple-element.16), channel_id=1, source_target_pairs={{0,5},{1,4},{2,7},{3,6},{4,1},{5,0},{6,3},{7,2},{8,13},{9,12},{10,... | collective-permute-start | bytes 3145736 | tf_op jit(solution)/shard_map/ppermute | solution.py:29
  122.9 65.5 %copy-start = (f32[512,4,128]{2,0,1:T(8,128)}, f32[512,4,128]{2,0,1:T(8,128)S(1)}, u32[]{:S(2)}) copy-start(f32[512,4,128]{2,0,1:T(8,128)S(1)} %collective-permute-done) | copy-start | bytes 3145732
  122.9 138.6 %collective-permute-start.5 = (f32[512,4,128]{2,0,1:T(8,128)S(1)}, f32[512,4,128]{2,0,1:T(8,128)}, u32[]{:S(2)}, u32[]{:S(2)}) collective-permute-start(f32[512,4,128]{2,0,1:T(8,128)S(1)} %get-tuple-element.15), channel_id=1, source_target_pairs={{0,6},{1,7},{2,4},{3,5},{4,2},{5,3},{6,0},{7,1},{8,14},{9,15},{10,... | collective-permute-start | bytes 3145736 | tf_op jit(solution)/shard_map/ppermute | solution.py:29
  188.4 1.1 copy-start.2
  189.4 74.4 %collective-permute-start.6 = (f32[512,4,128]{2,0,1:T(8,128)S(1)}, f32[512,4,128]{2,0,1:T(8,128)}, u32[]{:S(2)}, u32[]{:S(2)}) collective-permute-start(f32[512,4,128]{2,0,1:T(8,128)S(1)} %get-tuple-element.14), channel_id=1, source_target_pairs={{0,7},{1,6},{2,5},{3,4},{4,3},{5,2},{6,1},{7,0},{8,15},{9,14},{10,... | collective-permute-start | bytes 3145736 | tf_op jit(solution)/shard_map/ppermute | solution.py:29
  199.1 284.9 %all-to-all-start = ((f32[512,32,128]{0,2,1:T(8,128)}), f32[512,32,128]{0,2,1:T(8,128)}, u32[]{:S(2)}, u32[]{:S(2)}) async-start(f32[512,32,128]{0,2,1:T(8,128)} %bitcast.117), calls=%async_computation | async-start | bytes 16777216 | tf_op jit(solution)/shard_map/all_to_all | solution.py:46
  204.1 490.2 %all-reduce.3.cloned.1.call-start = ((), (), s32[]{:S(2)}) async-start(), calls=%async_computation.1 | async-start | bytes 16777216 | tf_op jit(solution)/shard_map/psum | solution.py:77
  204.4 6.2 copy-start.1
  204.4 7.3 copy-start.3
  391.3 906.0 %all-reduce.5.cloned.1.call-start = ((), (), s32[]{:S(2)}) async-start(), calls=%async_computation.2 | async-start | bytes 16777216 | tf_op jit(solution)/shard_map/psum | solution.py:77
  814.0 4.5 collective-permute-start.7
  814.1 70.3 %collective-permute-start.8 = (f32[512,4,128]{2,0,1:T(8,128)S(1)}, f32[512,4,128]{2,0,1:T(8,128)S(1)}, u32[]{:S(2)}, u32[]{:S(2)}) collective-permute-start(f32[512,4,128]{2,0,1:T(8,128)S(1)} %get-tuple-element.12), channel_id=1, source_target_pairs={{0,2},{1,3},{2,0},{3,1},{4,6},{5,7},{6,4},{7,5},{8,10},{9,11},{10,... | collective-permute-start | bytes 3145736 | tf_op jit(solution)/shard_map/ppermute | solution.py:29
  815.6 90.2 %collective-permute-start.9 = (f32[512,4,128]{2,0,1:T(8,128)S(1)}, f32[512,4,128]{2,0,1:T(8,128)S(1)}, u32[]{:S(2)}, u32[]{:S(2)}) collective-permute-start(f32[512,4,128]{2,0,1:T(8,128)S(1)} %get-tuple-element.11), channel_id=1, source_target_pairs={{0,3},{1,2},{2,1},{3,0},{4,7},{5,6},{6,5},{7,4},{8,11},{9,10},{10,... | collective-permute-start | bytes 3145736 | tf_op jit(solution)/shard_map/ppermute | solution.py:29
  815.9 90.9 %collective-permute-start.10 = (f32[512,4,128]{2,0,1:T(8,128)S(1)}, f32[512,4,128]{2,0,1:T(8,128)S(1)}, u32[]{:S(2)}, u32[]{:S(2)}) collective-permute-start(f32[512,4,128]{2,0,1:T(8,128)S(1)} %get-tuple-element.10), channel_id=1, source_target_pairs={{0,4},{1,5},{2,6},{3,7},{4,0},{5,1},{6,2},{7,3},{8,12},{9,13},{10,... | collective-permute-start | bytes 3145736 | tf_op jit(solution)/shard_map/ppermute | solution.py:29
  818.3 135.7 %collective-permute-start.11 = (f32[512,4,128]{2,0,1:T(8,128)S(1)}, f32[512,4,128]{2,0,1:T(8,128)S(1)}, u32[]{:S(2)}, u32[]{:S(2)}) collective-permute-start(f32[512,4,128]{2,0,1:T(8,128)S(1)} %get-tuple-element.9), channel_id=1, source_target_pairs={{0,5},{1,4},{2,7},{3,6},{4,1},{5,0},{6,3},{7,2},{8,13},{9,12},{10,... | collective-permute-start | bytes 3145736 | tf_op jit(solution)/shard_map/ppermute | solution.py:29
  818.6 136.5 %collective-permute-start.12 = (f32[512,4,128]{2,0,1:T(8,128)S(1)}, f32[512,4,128]{2,0,1:T(8,128)S(1)}, u32[]{:S(2)}, u32[]{:S(2)}) collective-permute-start(f32[512,4,128]{2,0,1:T(8,128)S(1)} %get-tuple-element.8), channel_id=1, source_target_pairs={{0,6},{1,7},{2,4},{3,5},{4,2},{5,3},{6,0},{7,1},{8,14},{9,15},{10,... | collective-permute-start | bytes 3145736 | tf_op jit(solution)/shard_map/ppermute | solution.py:29
  884.4 71.7 %collective-permute-start.13 = (f32[512,4,128]{2,0,1:T(8,128)S(1)}, f32[512,4,128]{2,0,1:T(8,128)S(1)}, u32[]{:S(2)}, u32[]{:S(2)}) collective-permute-start(f32[512,4,128]{2,0,1:T(8,128)S(1)} %get-tuple-element.6), channel_id=1, source_target_pairs={{0,7},{1,6},{2,5},{3,4},{4,3},{5,2},{6,1},{7,0},{8,15},{9,14},{10,... | collective-permute-start | bytes 3145736 | tf_op jit(solution)/shard_map/ppermute | solution.py:29
Sparse Core Ops, SparseCore 0:
  391.4 302.8 all-reduce.2
  1082.6 214.6 all-reduce.4
